TPU v7x, 512 devices: a whole 4x8x8 slice. The times are simulated.
512 devices in a mesh: leaf: 32 (over z, x), group: 16 (over y, core).
Axes of the slice: x: 4, y: 8, z: 8, core: 2. Of those that a mesh axis runs over, the one named last changes fastest.
Arguments:
- low_solved: float32 [262144, 256], P(('group', 'leaf')), may hold values from -4 to 4, as said below
- low_basis: float32 [262144, 256], P(('group', 'leaf')), may hold values from -0.001933495 to 0.001933495, as said below
- upper_solved: float32 [262144, 512], P(('group', 'leaf')), may hold values from -4 to 4, as said below
- upper_basis: float32 [262144, 256], P(('group', 'leaf')), may hold values from -0.001171875 to 0.001171875, as said below
Outputs:
- pair_solved: float32 [262144, 256], P(('group', 'leaf'))
- next_solved: float32 [262144, 256], P(('group', 'leaf'))
Inputs may be any that keep to these rules, and one draw needn't show every extreme that they name: `low_solved`: independent entries of mean zero. `low_basis`: independent entries of mean zero. `upper_solved`: independent entries of mean zero. `upper_basis`: independent entries of mean zero.
All inputs are finite; a program needn't handle non-finite values.
Results may differ from a plain program's by a relative error of at most 0.0003.
Values sent between devices are 32-bit elements; how exact they have to be, the bound alone decides.
A program may use at most 64 MiB of HBM per device.

v0:
```python
import jax
import jax.numpy as jnp
from jax import lax
from jax.sharding import PartitionSpec as P

ITERS = 4


def partner(x, axis, stride):
    return lax.ppermute(x, axis, [(i, i ^ 1 << stride) for i in range(lax.axis_size(axis))])


def product(left, right):
    return jnp.dot(left, right, precision=lax.Precision.HIGHEST, preferred_element_type=jnp.float32)


def transposed_product(left, right):
    return lax.dot_general(
        left,
        right,
        (((0,), (0,)), ((), ())),
        precision=lax.Precision.HIGHEST,
        preferred_element_type=jnp.float32,
    )


def jacobi(couple_first, rhs_first, couple_second, rhs_second):
    update_first = jnp.zeros(rhs_second.shape, jnp.float32)
    update_second = jnp.zeros(rhs_first.shape, jnp.float32)
    for sweep_index in range(ITERS):
        update_first, update_second = (
            rhs_second - product(couple_second, update_second),
            rhs_first - product(couple_first, update_first),
        )
    return (update_first, update_second)


def body(low_solved, low_basis, upper_solved, upper_basis):
    rank_width = low_solved.shape[1]
    leaves = lax.axis_size("leaf")
    half_index = lax.axis_index("leaf") // (leaves // 2)
    slot_mask = (jnp.arange(2) == half_index).astype(jnp.float32)
    joined = jnp.concatenate([low_solved, upper_solved], axis=1)
    local_terms = transposed_product(low_basis, joined)
    totals = lax.psum(slot_mask[:, None, None] * local_terms[None], "leaf")
    first_half = totals[0]
    second_half = totals[1]
    update_first, update_second = jacobi(
        first_half[:, :rank_width],
        first_half[:, rank_width:],
        second_half[:, :rank_width],
        second_half[:, rank_width:],
    )
    own_update = jnp.where(half_index == 0, update_first, update_second)
    middle = upper_solved - product(low_solved, own_update)
    group_total = lax.psum(transposed_product(upper_basis, middle), "leaf")
    pair_solved = middle[:, :rank_width]
    sibling = partner(group_total, "group", 0)
    parity = lax.axis_index("group") % 2
    first_group = jnp.where(parity == 0, group_total, sibling)
    second_group = jnp.where(parity == 0, sibling, group_total)
    pair_first, pair_second = jacobi(
        first_group[:, :rank_width],
        first_group[:, rank_width:],
        second_group[:, :rank_width],
        second_group[:, rank_width:],
    )
    pair_update = jnp.where(parity == 0, pair_first, pair_second)
    next_solved = middle[:, rank_width:] - product(pair_solved, pair_update)
    return (pair_solved, next_solved)


def solution(mesh):
    return jax.shard_map(
        body,
        mesh=mesh,
        in_specs=(
            P(("group", "leaf"), None),
            P(("group", "leaf"), None),
            P(("group", "leaf"), None),
            P(("group", "leaf"), None),
        ),
        out_specs=(P(("group", "leaf"), None), P(("group", "leaf"), None)),
        check_vma=False,
    )
```

profile of v0, /device:TPU:1, one launch (start us, length us, event | category | flops | bytes accessed | tf_op | source)
XLA Modules:
  0.0 367.2 jit_solution(1575446684602732130)
XLA Ops:
  7.2 0.0 copy-start
  7.2 0.0 all-reduce.3.cloned.1.call-start
  7.3 1.0 copy-done
  8.2 4.0 %fusion.5 = f32[256,768]{0,1:T(8,128)S(1)} fusion(f32[512,256]{1,0:T(8,128)S(1)} %copy-done, f32[512,512]{1,0:T(8,128)} %param.6, f32[512,256]{1,0:T(8,128)} %param.4), kind=kOutput, calls=%fused_computation.6 | convolution fusion | flops 1208352768 | bytes 2883584 | tf_op jit(solution)/shard_map/dot_general | solution.py:18
  12.2 0.3 copy.6
  12.5 0.0 copy-start.1
  12.5 1.3 broadcast_multiply_fusion
  13.8 0.0 all-reduce.3.cloned.1.call-update
  13.8 0.0 all-reduce.5.cloned.1.call-start
  13.9 0.1 copy-done.1
  14.0 0.3 copy.7
  14.3 164.7 %all-reduce.3.cloned.1.call-done = f32[2,256,768]{2,1,0:T(8,128)} async-done(((f32[2,256,768]{2,1,0:T(8,128)}), f32[2,256,768]{2,1,0:T(8,128)}) %all-reduce.3.cloned.1.call-update) | async-done | bytes 1572880 | tf_op jit(solution)/shard_map/psum | solution.py:45
  179.0 1.5 slice_bitcast_fusion.1
  180.5 0.6 convolution_subtract_fusion.4
  181.0 0.6 convolution_subtract_fusion.8
  181.6 0.6 convolution_subtract_fusion.3
  182.2 0.6 convolution_subtract_fusion.2
  182.9 0.6 convolution_subtract_fusion.7
  183.5 0.6 convolution_subtract_fusion.6
  184.1 0.0 copy-start.2
  184.1 0.6 convolution_subtract_fusion.5
  184.8 0.6 fusion.8
  185.4 0.0 copy-done.2
  185.4 0.0 copy-start.4
  185.4 1.9 fusion.4
  187.3 0.0 copy-done.4
  187.3 1.8 convolution_bitcast_fusion.1
  189.1 0.0 all-reduce.5.cloned.1.call-update
  189.1 157.5 %all-reduce.5.cloned.1.call-done = f32[256,512]{0,1:T(8,128)} async-done(((f32[256,512]{0,1:T(8,128)}), f32[256,512]{0,1:T(8,128)}) %all-reduce.5.cloned.1.call-update) | async-done | bytes 524304 | tf_op jit(solution)/shard_map/psum | solution.py:56
  346.6 0.0 copy-start.3
  346.6 7.2 %collective-permute-start = (f32[256,512]{0,1:T(8,128)}, f32[256,512]{0,1:T(8,128)S(1)}, u32[]{:S(2)}, u32[]{:S(2)}) collective-permute-start(f32[256,512]{0,1:T(8,128)} %all-reduce.5.cloned.1.call-done), channel_id=1, source_target_pairs={{0,1},{1,0},{2,3},{3,2},{4,5},{5,4},{6,7},{7,6},{8,9},{9,8},{10,11... | collective-permute-start | bytes 1572872 | tf_op jit(solution)/shard_map/ppermute | solution.py:10
  353.9 1.0 copy.9
  354.9 0.5 collective-permute-done
  355.4 0.0 copy-done.3
  355.4 0.1 broadcast_select_fusion
  355.5 0.4 convolution_subtract_fusion.16
  355.9 0.4 convolution_subtract_fusion.12
  356.3 0.4 convolution_subtract_fusion.15
  356.7 0.4 convolution_subtract_fusion.14
  357.1 0.4 convolution_subtract_fusion.11
  357.5 0.4 convolution_subtract_fusion.10
  357.9 0.4 convolution_subtract_fusion.9
  358.3 0.4 fusion.9
  358.7 0.6 convolution_subtract_fusion
  359.3 1.0 copy.10
  (2 shorter events, 0.0 us)
Async XLA Ops:
  7.2 1.0 copy-start
  7.2 171.8 %all-reduce.3.cloned.1.call-start = ((), (), s32[]{:S(2)}) async-start(), calls=%async_computation | async-start | bytes 3145728 | tf_op jit(solution)/shard_map/psum | solution.py:45
  12.5 1.5 copy-start.1
  13.8 332.8 %all-reduce.5.cloned.1.call-start = ((), (), s32[]{:S(2)}) async-start(), calls=%async_computation.1 | async-start | bytes 1048576 | tf_op jit(solution)/shard_map/psum | solution.py:56
  184.1 1.3 copy-start.2
  185.4 1.9 copy-start.4
  346.6 8.8 %copy-start.3 = (f32[256,512]{0,1:T(8,128)S(1)}, f32[256,512]{0,1:T(8,128)}, u32[]{:S(2)}) copy-start(f32[256,512]{0,1:T(8,128)} %all-reduce.5.cloned.1.call-done) | copy-start | bytes 1572868
  346.6 8.8 %collective-permute-start = (f32[256,512]{0,1:T(8,128)}, f32[256,512]{0,1:T(8,128)S(1)}, u32[]{:S(2)}, u32[]{:S(2)}) collective-permute-start(f32[256,512]{0,1:T(8,128)} %all-reduce.5.cloned.1.call-done), channel_id=1, source_target_pairs={{0,1},{1,0},{2,3},{3,2},{4,5},{5,4},{6,7},{7,6},{8,9},{9,8},{10,11... | collective-permute-start | bytes 1572872 | tf_op jit(solution)/shard_map/ppermute | solution.py:10
Sparse Core Ops, SparseCore 0:
  13.9 165.0 all-reduce.2
  189.2 157.3 all-reduce.4
where the time goes:
time: 367 us
  waiting for transfers between devices  323 us (88%)
  matrix products  16.3 us (4%)
  between operations  14.3 us (4%)
  starting transfers between devices  7.31 us (2%)
  local copies, waits for them, and re-layouts  5.18 us (1%)
    psum x1, waiting for transfers between devices, body(): totals = lax.psum(slot_mask[:, None, None] * local_terms[None], 'leaf')  165 us
    psum x1, waiting for transfers between devices, body(): group_total = lax.psum(transposed_product(upper_basis, middle), 'leaf')  157 us
    dot_general x18, matrix products, product(): jnp.dot(left, right, precision=lax.Precision.HIGHEST, preferred_element_t...  10.5 us
  transfers between devices with their start and end apart: 3, of which 3 were waited for; matrix products, arithmetic and copies ran while one was open for 0% of the time, Pallas kernels for 0%

commit v1 on v0

v1 whole, which is shorter than its diff:
```python
import jax
import jax.numpy as jnp
from jax import lax
from jax.experimental import pallas as pl
from jax.experimental.pallas import tpu as pltpu
from jax.sharding import PartitionSpec as P

MESH = pl.DeviceIdType.MESH
NX = 4
NZ = 8
F32 = jnp.float32
BF16 = jnp.bfloat16
N_MESSAGES = 80


def split(value):
    high = value.astype(BF16)
    return high, (value - high.astype(F32)).astype(BF16)


def dot3(left, right):
    left_high, left_low = left
    right_high, right_low = right
    total = jnp.dot(left_high, right_high, preferred_element_type=F32)
    total += jnp.dot(left_high, right_low, preferred_element_type=F32)
    return total + jnp.dot(left_low, right_high, preferred_element_type=F32)


def kernel(
    y_hbm, v_hbm, z_hbm, w_hbm, pair_hbm, next_hbm,
    y_ref, v_ref, z_ref, w_ref, pair_ref, next_ref,
    part_g, part_p, part_q, part_s,
    first_g, first_p, first_q, first_s,
    second_g, second_p, second_q, second_s,
    slice_g, slice_p, slice_q, slice_s,
    peers_g, peers_p, peers_q, peers_s,
    full_g, full_p, table_q, table_s,
    full_u, full_e, sibling_e,
    local_sem, send_sem, recv_sem,
):
    rank = y_ref.shape[1]
    lanes = rank // 2
    rows_l = rank // NX // 4
    rows_q = rank // 4
    leaf = lax.axis_index("leaf")
    group = lax.axis_index("group")
    z, x = leaf // NX, leaf % NX
    half, place = z // 4, z % 4
    flip = x + 1 - 2 * (x % 2)
    mirror = NX - 1 - x
    right, left = (x + 1) % NX, (x + NX - 1) % NX
    up, down = (z + 1) % NZ, (z + NZ - 1) % NZ
    sibling = group + 1 - 2 * (group % 2)

    copies = []
    for index, (source, target) in enumerate(((v_hbm, v_ref), (y_hbm, y_ref), (w_hbm, w_ref), (z_hbm, z_ref))):
        copy = pltpu.make_async_copy(source, target, local_sem.at[index])
        copy.start()
        copies.append(copy)

    barrier = pltpu.get_barrier_semaphore()
    partners = [(z, right), (z, left), (up, x), (down, x)]
    partners += [(half * 4 + (place + d) % 4, x) for d in (1, 2, 3)]
    for pz, px in partners:
        pl.semaphore_signal(barrier, inc=1, device_id={"leaf": pz * NX + px}, device_id_type=MESH)
    pl.semaphore_signal(barrier, inc=1, device_id={"group": sibling}, device_id_type=MESH)

    sent = []

    def send(source, target, device):
        index = len(sent)
        copy = pltpu.make_async_remote_copy(
            src_ref=source,
            dst_ref=target,
            send_sem=send_sem.at[index],
            recv_sem=recv_sem.at[index],
            device_id=device,
            device_id_type=MESH,
        )
        copy.start()
        sent.append(copy)
        return copy

    def at(pz, px):
        return {"leaf": pz * NX + px}

    def reduce_flow(colour, part, first, second, sliced, peers, table):
        if colour == 0:
            one, two = flip, mirror
            keep = 2 * ((x + 1) // 2 % 2)
            own, away = (x + 1) % NX, (mirror + 1) % NX
        else:
            one, two = mirror, flip
            keep = 2 * (x // 2)
            own, away = x, flip
        step_one = send(part.at[pl.ds(2 - keep, 2)], first, at(z, one))
        yield
        step_one.wait_recv()
        part[away] = part[away] + first[away - keep]
        step_two = send(part.at[away], second, at(z, two))
        sliced[...] = part[own] + first[own - keep]
        yield
        step_two.wait_recv()
        sliced[...] = sliced[...] + second[...]
        waits = []
        for d in (1, 2, 3):
            other = (place + d) % 4
            waits.append(send(sliced.at[other], peers.at[d - 1], at(half * 4 + other, x)))
        yield
        for wait in waits:
            wait.wait_recv()
        table[z] = (sliced[place] + peers[0]) + (peers[1] + peers[2])
        n_up, n_down = (4, 3) if colour == 0 else (3, 4)
        going_up = send(table.at[z], table.at[z], at(up, x))
        going_down = send(table.at[z], table.at[z], at(down, x))
        for k in range(1, 5):
            yield
            if k <= n_up:
                going_up.wait_recv()
                if k < n_up:
                    slot = (z + NZ - k) % NZ
                    going_up = send(table.at[slot], table.at[slot], at(up, x))
            if k <= n_down:
                going_down.wait_recv()
                if k < n_down:
                    slot = (z + k) % NZ
                    going_down = send(table.at[slot], table.at[slot], at(down, x))

    def gather_x(full):
        n = full.shape[1] // 2
        to_right = send(full.at[x], full.at[x], at(z, right))
        to_left = send(full.at[x], full.at[x], at(z, left))
        yield
        to_right.wait_recv()
        far_right = send(full.at[left, pl.ds(0, n)], full.at[left, pl.ds(0, n)], at(z, right))
        to_left.wait_recv()
        far_left = send(full.at[right, pl.ds(n, n)], full.at[right, pl.ds(n, n)], at(z, left))
        yield
        far_right.wait_recv()
        far_left.wait_recv()

    def run(flow):
        return next(flow, None)

    copies[0].wait()
    left_v = split(v_ref[...].T)
    copies[1].wait()
    y_parts = split(y_ref[...])

    def put_l(part, value, shift):
        for s in range(NX):
            for j in range(4):
                row = s * 4 * rows_l + j * rows_l
                part[(s + shift) % NX, j, pl.ds(0, rows_l)] = value[row : row + rows_l, :lanes]
                part[(s + shift) % NX, j, pl.ds(rows_l, rows_l)] = value[row : row + rows_l, lanes:]

    def put_q(part, value, slots):
        for n, slot in enumerate(slots):
            for j in range(4):
                part[slot, j] = value[j * rows_q : (j + 1) * rows_q, n * lanes : (n + 1) * lanes]

    put_l(part_g, dot3(left_v, y_parts), 1)
    pl.semaphore_wait(barrier, len(partners) + 1)
    flow_g = reduce_flow(0, part_g, first_g, second_g, slice_g, peers_g, full_g.at[x])
    run(flow_g)
    copies[2].wait()
    left_w = split(w_ref[...].T)
    put_l(part_p, dot3(left_w, y_parts), 0)
    flow_p = reduce_flow(1, part_p, first_p, second_p, slice_p, peers_p, full_p.at[x])
    run(flow_p)
    copies[3].wait()
    z_pair = split(z_ref[:, :rank])
    z_next = split(z_ref[:, rank:])
    put_q(part_q, dot3(left_v, z_pair), (1, 2))
    put_q(part_q, dot3(left_v, z_next), (3, 0))
    flow_q = reduce_flow(0, part_q, first_q, second_q, slice_q, peers_q, table_q)
    run(flow_q)
    put_q(part_s, dot3(left_w, z_pair), (0, 1))
    put_q(part_s, dot3(left_w, z_next), (2, 3))
    flow_s = reduce_flow(1, part_s, first_s, second_s, slice_s, peers_s, table_s)
    run(flow_s)

    small, large = (flow_g, flow_p), (flow_q, flow_s)
    for flow in small:
        run(flow)
    for flow in small:
        run(flow)
    for flow in large:
        run(flow)
    for flow in small:
        run(flow)
    for flow in large:
        run(flow)
    for step in range(4):
        for flow in small:
            run(flow)
        if step == 1:
            for flow in large:
                run(flow)
    gathers = gather_x(full_g), gather_x(full_p)
    for flow in gathers:
        run(flow)
    for step in range(2):
        for flow in large:
            run(flow)
    for flow in gathers:
        run(flow)
    for step in range(2):
        for flow in large:
            run(flow)
    for flow in gathers:
        run(flow)

    def whole(full, h):
        block = full[:, pl.ds(4 * h, 4)]
        halves = [block[:, :, n * rows_l : (n + 1) * rows_l].reshape(rank, lanes) for n in range(2)]
        return jnp.concatenate(halves, axis=1)

    mine, others = half, 1 - half
    g_own, g_other = split(whole(full_g, mine)), split(whole(full_g, others))
    q_own = table_q[pl.ds(4 * mine, 4)].reshape(rank, lanes)
    q_other = table_q[pl.ds(4 * others, 4)].reshape(rank, lanes)
    u_own, u_other = q_other, q_own
    for sweep in range(3):
        u_own, u_other = (
            q_other - dot3(g_other, split(u_other)),
            q_own - dot3(g_own, split(u_own)),
        )
    full_u[x] = u_own.reshape(4, rows_q, lanes)
    flow_u = gather_x(full_u)
    run(flow_u)
    p_own, p_other = split(whole(full_p, mine)), split(whole(full_p, others))
    total_s = (table_s[pl.ds(0, 4)] + table_s[pl.ds(4, 4)]).reshape(rank, lanes)
    e_slice = total_s - dot3(p_own, split(u_own)) - dot3(p_other, split(u_other))
    full_e[x] = e_slice.reshape(4, rows_q, lanes)
    across = {"group": sibling}
    flow_e = gather_x(full_e)
    run(flow_e)
    shared = [send(full_e.at[x], sibling_e.at[x], across)]
    run(flow_u)
    run(flow_e)
    for slot in (left, right):
        shared.append(send(full_e.at[slot], sibling_e.at[slot], across))
    run(flow_u)

    y_parts = split(y_ref[...])

    def joined(full, first_slot):
        return jnp.concatenate([full[first_slot + n].reshape(rank, lanes) for n in range(2)], axis=1)

    pair = z_ref[:, :rank] - dot3(y_parts, split(joined(full_u, 0)))
    pair_ref[...] = pair
    pair_out = pltpu.make_async_copy(pair_ref, pair_hbm, local_sem.at[4])
    pair_out.start()
    middle_next = z_ref[:, rank:] - dot3(y_parts, split(joined(full_u, 2)))
    run(flow_e)
    far = (x + 2) % NX
    shared.append(send(full_e.at[far], sibling_e.at[far], across))
    for copy in shared:
        copy.wait_recv()
    b_own, r_own = split(joined(full_e, 0)), joined(full_e, 2)
    b_sibling, r_sibling = split(joined(sibling_e, 0)), joined(sibling_e, 2)
    update = r_own
    update = r_sibling - dot3(b_sibling, split(update))
    update = r_own - dot3(b_own, split(update))
    update = r_sibling - dot3(b_sibling, split(update))
    next_ref[...] = middle_next - dot3(split(pair), split(update))
    next_out = pltpu.make_async_copy(next_ref, next_hbm, local_sem.at[5])
    next_out.start()
    for copy in sent:
        copy.wait_send()
    pair_out.wait()
    next_out.wait()


def body(low_solved, low_basis, upper_solved, upper_basis):
    rows, rank = low_solved.shape
    lanes, rows_l, rows_q = rank // 2, rank // NX // 4, rank // 4
    heights = (2 * rows_l, 2 * rows_l, rows_q, rows_q)

    def blocks(*lead):
        return [pltpu.VMEM((*lead, height, lanes), F32) for height in heights]

    scratch = [
        pltpu.VMEM((rows, rank), F32),
        pltpu.VMEM((rows, rank), F32),
        pltpu.VMEM((rows, 2 * rank), F32),
        pltpu.VMEM((rows, rank), F32),
        pltpu.VMEM((rows, rank), F32),
        pltpu.VMEM((rows, rank), F32),
        *blocks(NX, 4),
        *blocks(2, 4),
        *blocks(4),
        *blocks(4),
        *blocks(3),
        pltpu.VMEM((NX, NZ, 2 * rows_l, lanes), F32),
        pltpu.VMEM((NX, NZ, 2 * rows_l, lanes), F32),
        pltpu.VMEM((NZ, rows_q, lanes), F32),
        pltpu.VMEM((NZ, rows_q, lanes), F32),
        pltpu.VMEM((NX, 4, rows_q, lanes), F32),
        pltpu.VMEM((NX, 4, rows_q, lanes), F32),
        pltpu.VMEM((NX, 4, rows_q, lanes), F32),
        pltpu.SemaphoreType.DMA((6,)),
        pltpu.SemaphoreType.DMA((N_MESSAGES,)),
        pltpu.SemaphoreType.DMA((N_MESSAGES,)),
    ]
    out = jax.ShapeDtypeStruct((rows, rank), F32)
    return pl.pallas_call(
        kernel,
        out_shape=(out, out),
        in_specs=[pl.BlockSpec(memory_space=pl.ANY)] * 4,
        out_specs=[pl.BlockSpec(memory_space=pl.ANY)] * 2,
        scratch_shapes=scratch,
        compiler_params=pltpu.CompilerParams(collective_id=0, has_side_effects=True, vmem_limit_bytes=60 * 2**20),
        name="lowrank_level",
    )(low_solved, low_basis, upper_solved, upper_basis)


def solution(mesh):
    spec = P(("group", "leaf"), None)
    return jax.shard_map(
        body, mesh=mesh, in_specs=(spec,) * 4, out_specs=(spec,) * 2, check_vma=False
    )
```

time: 367 us -> 71.2 us (0.19)
  waiting for transfers between devices: 323 us -> 0 us
  Pallas kernels: 0 us -> 67.6 us
  matrix products: 16.3 us -> 0 us
  between operations: 14.3 us -> 0.65 us
  starting transfers between devices: 7.31 us -> 0 us
    psum x2 -> x0, waiting for transfers between devices: 322 us -> none  [the longest x1 165 us: body(): totals = lax.psum(slot_mask[:, None, None] * local_terms[None], 'leaf')]
    pallas_call x0 -> x1, Pallas kernels: none -> 67.6 us  [body(): pl.pallas_call(kernel, out_shape=(out, out), in_specs=[pl.BlockSpec(memor...]
    dot_general x20 -> x0, matrix products: 16.3 us -> none  [the longest x18 10.5 us: product(): jnp.dot(left, right, precision=lax.Precision.HIGHEST, preferred_element_t...]
    ppermute x1 -> x0, starting transfers between devices: 7.23 us -> none  [partner(): lax.ppermute(x, axis, [(i, i ^ 1 << stride) for i in range(lax.axis_size(...]
  transfers between devices with their start and end apart: 3 -> 0, of which waited for: 3 -> 0; matrix products, arithmetic and copies ran while one was open for 0% -> 0% of each run, Pallas kernels for 0% -> 0%
where the time goes in v1:
time: 71.2 us; the launch traced here: 71 us
  Pallas kernels  67.6 us (95%)
  local copies, waits for them, and re-layouts  2.72 us (4%)
    pallas_call x1, Pallas kernels, body(): pl.pallas_call(kernel, out_shape=(out, out), in_specs=[pl.BlockSpec(memor...  67.6 us
    unnamed x4, local copies, waits for them, and re-layouts  2.72 us

profile of v1, /device:TPU:1, one launch (start us, length us, event | category | flops | bytes accessed | tf_op | source)
XLA Modules:
  0.0 71.0 jit_solution(6275684579476549481)
XLA Ops:
  0.6 67.6 %lowrank_level.1 = (f32[512,256]{1,0:T(8,128)}, f32[512,256]{1,0:T(8,128)}) custom-call(f32[512,256]{1,0:T(8,128)} %y_hbm.1, f32[512,256]{1,0:T(8,128)} %v_hbm.1, f32[512,512]{1,0:T(8,128)} %z_hbm.1, f32[512,256]{1,0:T(8,128)} %w_hbm.1), custom_call_target="tpu_custom_call" | custom-call | tf_op jit(solution)/shard_map/lowrank_level/pallas_call | solution.py:308
  68.3 0.0 copy-start
  68.3 1.9 %copy.8 = f32[512,256]{1,0:T(8,128)} copy(f32[512,256]{1,0:T(8,128)} %get-tuple-element.4) | data formatting | bytes 1048576
  70.2 0.0 copy-done
  70.2 0.8 %copy.9 = f32[512,256]{1,0:T(8,128)} copy(f32[512,256]{1,0:T(8,128)S(1)} %copy-done) | data formatting | bytes 1048576
Async XLA Ops:
  68.3 1.9 %copy-start = (f32[512,256]{1,0:T(8,128)S(1)}, f32[512,256]{1,0:T(8,128)}, u32[]{:S(2)}) copy-start(f32[512,256]{1,0:T(8,128)} %get-tuple-element.5) | copy-start | bytes 1572868

commit v2 on v1

v2 whole, which is shorter than its diff:
```python
import jax
import jax.numpy as jnp
from jax import lax
from jax.experimental import pallas as pl
from jax.experimental.pallas import tpu as pltpu
from jax.sharding import PartitionSpec as P

MESH = pl.DeviceIdType.MESH
NX = 4
NZ = 8
F32 = jnp.float32
BF16 = jnp.bfloat16
N_MESSAGES = 176
X_DIRECT = ""
Z_DIRECT = ""
G_DIRECT = "g"
ORDER = (
    "CG", "xg", "CQ", "xq", "CP", "xg", "CS", "xp", "xq", "xs", "xg", "zg", "xp", "xq", "zq", "zg", "xs", "ag",
    "xp", "zp", "ag", "gn", "xs", "zs", "zp", "zq", "ap", "ag", "aq", "ap", "gn", "pn", "ap", "ag", "gr", "zs",
    "as", "aq", "ap", "pr", "aq", "pn", "as", "as", "pr", "gr", "aq", "U", "as", "pr", "pn", "E", "fu", "ef",
    "en", "fu", "M",
)


def split(value):
    high = value.astype(BF16)
    return high, (value - high.astype(F32)).astype(BF16)


def dot3(left, right):
    left_high, left_low = left
    right_high, right_low = right
    total = jnp.dot(left_high, right_high, preferred_element_type=F32)
    total += jnp.dot(left_high, right_low, preferred_element_type=F32)
    return total + jnp.dot(left_low, right_high, preferred_element_type=F32)


def kernel(
    y_hbm, v_hbm, z_hbm, w_hbm, pair_hbm, next_hbm,
    y_ref, v_ref, z_ref, w_ref, pair_ref, next_ref,
    part_g, part_p, part_q, part_s,
    first_g, first_p, first_q, first_s,
    second_g, second_p, second_q, second_s,
    slice_g, slice_p, slice_q, slice_s,
    peers_g, peers_p, peers_q, peers_s,
    full_g, full_p, table_q, table_s,
    full_u, full_e, sibling_e,
    local_sem, send_sem, recv_sem,
):
    rank = y_ref.shape[1]
    lanes = rank // 2
    rows_l = rank // NX // 4
    rows_q = rank // 4
    leaf = lax.axis_index("leaf")
    group = lax.axis_index("group")
    z, x = leaf // NX, leaf % NX
    half, place = z // 4, z % 4
    flip = x + 1 - 2 * (x % 2)
    mirror = NX - 1 - x
    right, left = (x + 1) % NX, (x + NX - 1) % NX
    sibling = group + 1 - 2 * (group % 2)

    copies = []
    for index, (source, target) in enumerate(((v_hbm, v_ref), (y_hbm, y_ref), (z_hbm, z_ref), (w_hbm, w_ref))):
        copy = pltpu.make_async_copy(source, target, local_sem.at[index])
        if index < 2:
            copy.start()
        copies.append(copy)

    barrier = pltpu.get_barrier_semaphore()
    partners = [(z, right), (z, left), (z, (x + 2) % NX)] + [((z + d + NZ) % NZ, x) for d in (1, -1, 2, -2, 3, -3, 4)]
    for pz, px in partners:
        pl.semaphore_signal(barrier, inc=1, device_id={"leaf": pz * NX + px}, device_id_type=MESH)
    pl.semaphore_signal(barrier, inc=1, device_id={"group": sibling}, device_id_type=MESH)

    sent = []

    def send(source, target, device):
        index = len(sent)
        copy = pltpu.make_async_remote_copy(
            src_ref=source,
            dst_ref=target,
            send_sem=send_sem.at[index],
            recv_sem=recv_sem.at[index],
            device_id=device,
            device_id_type=MESH,
        )
        copy.start()
        sent.append(copy)
        return copy

    def at(pz, px):
        return {"leaf": pz * NX + px}

    def scatter_x(colour, part, first, second, sliced, n, direct):
        if colour == 0:
            one, two = flip, mirror
            keep = 2 * ((x + 1) // 2 % 2)
            own, away = (x + 1) % NX, (mirror + 1) % NX
        else:
            one, two = mirror, flip
            keep = 2 * (x // 2)
            own, away = x, flip
        if direct:
            copies_in = []
            for d, target in ((1, first.at[colour, 0]), (3, first.at[colour, 1]), (2, second.at[colour])):
                px = (x + d) % NX
                copies_in.append(send(part.at[colour, px if colour else (px + 1) % NX], target, at(z, px)))
            yield
            for copy in copies_in:
                copy.wait_recv()
            sliced[:, n] = (part[colour, own] + first[colour, 0]) + (first[colour, 1] + second[colour])
            return
        step_one = send(part.at[colour, pl.ds(2 - keep, 2)], first.at[colour], at(z, one))
        yield
        step_one.wait_recv()
        part[colour, away] = part[colour, away] + first[colour, away - keep]
        step_two = send(part.at[colour, away], second.at[colour], at(z, two))
        sliced[:, n] = part[colour, own] + first[colour, own - keep]
        yield
        step_two.wait_recv()
        sliced[:, n] = sliced[:, n] + second[colour]

    def scatter_z(sliced, peers, put):
        waits = []
        for d in (1, 2, 3):
            other = (place + d) % 4
            waits.append(send(sliced.at[other], peers.at[d - 1], at(half * 4 + other, x)))
        yield
        for wait in waits:
            wait.wait_recv()
        put((sliced[place] + peers[0]) + (peers[1] + peers[2]))

    def gather_z(table, far, slots, direct):
        def pass_on(k, to):
            here, there = slots(k, to)
            return send(table(here), table(there), at((z + to + NZ) % NZ, x))

        near = [pass_on(0, to) for to in (1, -1)]
        second = [pass_on(0, to) for to in (2, -2)]
        if direct:
            second += [pass_on(0, to) for to in (3, -3, 4 * far)]
            yield
            for copy in near:
                copy.wait_recv()
            yield
            yield
            for copy in second:
                copy.wait_recv()
            return
        yield
        for copy in near:
            copy.wait_recv()
        third = [pass_on(-1, 2), pass_on(1, -2)]
        yield
        for copy in second:
            copy.wait_recv()
        third.append(pass_on(-2 * far, 2 * far))
        yield
        for copy in third:
            copy.wait_recv()

    def gather_x(full, pieces, to_right_far, to_left_far, direct=False):
        if direct:
            moves = [send(full.at[x, p], full.at[x, p], at(z, px)) for px in (right, left, (x + 2) % NX) for p in pieces]
            yield
            for copy in moves:
                copy.wait_recv()
            return
        to_right = [send(full.at[x, p], full.at[x, p], at(z, right)) for p in pieces]
        to_left = [send(full.at[x, p], full.at[x, p], at(z, left)) for p in pieces]
        yield
        for copy in to_right:
            copy.wait_recv()
        far_right = send(full.at[left, to_right_far], full.at[left, to_right_far], at(z, right))
        for copy in to_left:
            copy.wait_recv()
        far_left = send(full.at[right, to_left_far], full.at[right, to_left_far], at(z, left))
        yield
        far_right.wait_recv()
        far_left.wait_recv()

    def run(*flows):
        for flow in flows:
            next(flow, None)

    def absolute(k, to):
        slot = (z + k + NZ) % NZ
        return slot, slot

    def relative(k, to):
        return 4 + k, 4 + k - to

    def put_full(full):
        def put(value):
            full[x, 4] = value.reshape(full.shape[2:])
        return put

    def put_table(table):
        def put(value):
            table[z] = value.reshape(table.shape[1:])
        return put

    def put_l(part, value):
        for n in range(2):
            for s in range(NX):
                for j in range(4):
                    row = s * 4 * rows_l + j * rows_l
                    slot = (s + 1) % NX if n == 0 else s
                    part[n, slot, j] = value[row : row + rows_l, n * lanes : (n + 1) * lanes]

    def put_q(part, value, slices):
        for m, s in enumerate(slices):
            for j in range(4):
                for n in range(2):
                    slot = (s + 1) % NX if n == 0 else s
                    row = j * rows_q + n * (rows_q // 2)
                    part[n, slot, j] = value[row : row + rows_q // 2, m * lanes : (m + 1) * lanes]

    def scatters(part, first, second, sliced, name):
        return [scatter_x(n, part, first, second, sliced, n, name in X_DIRECT) for n in range(2)]

    xg = scatters(part_g, first_g, second_g, slice_g, "g")
    xp = scatters(part_p, first_p, second_p, slice_p, "p")
    xq = scatters(part_q, first_q, second_q, slice_q, "q")
    xs = scatters(part_s, first_s, second_s, slice_s, "s")
    zg = scatter_z(slice_g, peers_g, put_full(full_g))
    zp = scatter_z(slice_p, peers_p, put_full(full_p))
    zq = scatter_z(slice_q, peers_q, put_table(table_q))
    zs = scatter_z(slice_s, peers_s, put_table(table_s))
    ag = gather_z(lambda slot: full_g.at[x, slot], 1, relative, "g" in Z_DIRECT)
    ap = gather_z(lambda slot: full_p.at[x, slot], 1, relative, "p" in Z_DIRECT)
    aq = gather_z(lambda slot: table_q.at[slot], -1, absolute, "q" in Z_DIRECT)
    as_ = gather_z(lambda slot: table_s.at[slot], -1, absolute, "s" in Z_DIRECT)

    def near(full, name):
        return gather_x(full, [pl.ds(3, 3)], pl.ds(3, 1), pl.ds(4, 2), name in G_DIRECT)

    def rest(full, name):
        return gather_x(full, [pl.ds(0, 3), pl.ds(6, 2)], pl.ds(0, 3), pl.ds(6, 2), name in G_DIRECT)

    def blocks(full):
        return gather_x(full, [pl.ds(0, 4)], pl.ds(0, 2), pl.ds(2, 2))

    held = {}

    def whole(full, h):
        halves = [[], []]
        for s in range(NX):
            for j in range(4):
                slot = (4 * h + j - z + 4 + NZ) % NZ
                for n in range(2):
                    halves[n].append(full[s, slot, pl.ds(n * rows_l, rows_l)])
        return jnp.concatenate([jnp.concatenate(rows, axis=0) for rows in halves], axis=1)

    def joined(full, first_slot):
        return jnp.concatenate([full[first_slot + n].reshape(rank, lanes) for n in range(2)], axis=1)

    mine, others = half, 1 - half
    across = {"group": sibling}
    shared = []

    def compute_g():
        copies[0].wait()
        held["v"] = split(v_ref[...].T)
        copies[1].wait()
        copies[2].start()
        copies[3].start()
        held["y"] = split(y_ref[...])
        put_l(part_g, dot3(held["v"], held["y"]))
        pl.semaphore_wait(barrier, len(partners) + 1)

    def compute_q():
        copies[2].wait()
        held["pair"] = split(z_ref[:, :rank])
        put_q(part_q, dot3(held["v"], held["pair"]), (0, 1))
        held["next"] = split(z_ref[:, rank:])
        put_q(part_q, dot3(held["v"], held["next"]), (2, 3))

    def compute_p():
        copies[3].wait()
        held["w"] = split(w_ref[...].T)
        put_l(part_p, dot3(held["w"], held["y"]))

    def compute_s():
        put_q(part_s, dot3(held["w"], held["pair"]), (0, 1))
        put_q(part_s, dot3(held["w"], held["next"]), (2, 3))

    flow_u = blocks(full_u)
    far = (x + 2) % NX

    def solve_u():
        g_own, g_other = split(whole(full_g, mine)), split(whole(full_g, others))
        q_own = table_q[pl.ds(4 * mine, 4)].reshape(rank, lanes)
        q_other = table_q[pl.ds(4 * others, 4)].reshape(rank, lanes)
        u_own, u_other = q_other, q_own
        for sweep in range(3):
            u_own, u_other = (
                q_other - dot3(g_other, split(u_other)),
                q_own - dot3(g_own, split(u_own)),
            )
        held["u"] = u_own, u_other
        full_u[x] = u_own.reshape(4, rows_q, lanes)
        run(flow_u)

    def solve_e():
        u_own, u_other = held["u"]
        p_own, p_other = split(whole(full_p, mine)), split(whole(full_p, others))
        total_s = (table_s[pl.ds(0, 4)] + table_s[pl.ds(4, 4)]).reshape(rank, lanes)
        e_slice = total_s - dot3(p_own, split(u_own)) - dot3(p_other, split(u_other))
        full_e[x] = e_slice.reshape(4, rows_q, lanes)
        held["e"] = [send(full_e.at[x], full_e.at[x], at(z, px)) for px in (right, left, far)]
        shared.append(send(full_e.at[x], sibling_e.at[x], across))

    def near_e():
        for copy, slot in zip(held["e"], (left, right)):
            copy.wait_recv()
            shared.append(send(full_e.at[slot], sibling_e.at[slot], across))

    def far_e():
        held["e"][2].wait_recv()
        shared.append(send(full_e.at[far], sibling_e.at[far], across))

    def middle():
        y_parts = split(y_ref[...])
        pair = z_ref[:, :rank] - dot3(y_parts, split(joined(full_u, 0)))
        pair_ref[...] = pair
        pair_out = pltpu.make_async_copy(pair_ref, pair_hbm, local_sem.at[4])
        pair_out.start()
        held["m"] = pair, z_ref[:, rank:] - dot3(y_parts, split(joined(full_u, 2))), pair_out

    actions = {
        "CG": compute_g, "CQ": compute_q, "CP": compute_p, "CS": compute_s,
        "U": solve_u, "E": solve_e, "fu": lambda: run(flow_u), "en": near_e, "ef": far_e, "M": middle,
    }
    flows = {
        "xg": xg, "xq": xq, "xp": xp, "xs": xs, "zg": [zg], "zq": [zq], "zp": [zp], "zs": [zs],
        "ag": [ag], "aq": [aq], "ap": [ap], "as": [as_],
        "gn": [near(full_g, "g")], "gr": [rest(full_g, "g")], "pn": [near(full_p, "p")], "pr": [rest(full_p, "p")],
    }
    for token in ORDER:
        if token in actions:
            actions[token]()
        else:
            run(*flows[token])

    for copy in shared:
        copy.wait_recv()
    pair, middle_next, pair_out = held["m"]
    b_own, r_own = split(joined(full_e, 0)), joined(full_e, 2)
    b_sibling, r_sibling = split(joined(sibling_e, 0)), joined(sibling_e, 2)
    update = r_own
    update = r_sibling - dot3(b_sibling, split(update))
    update = r_own - dot3(b_own, split(update))
    update = r_sibling - dot3(b_sibling, split(update))
    next_ref[...] = middle_next - dot3(split(pair), split(update))
    next_out = pltpu.make_async_copy(next_ref, next_hbm, local_sem.at[5])
    next_out.start()
    for copy in sent:
        copy.wait_send()
    pair_out.wait()
    next_out.wait()


def body(low_solved, low_basis, upper_solved, upper_basis):
    rows, rank = low_solved.shape
    lanes, rows_l, rows_q = rank // 2, rank // NX // 4, rank // 4
    heights = (rows_l, rows_l, rows_q // 2, rows_q // 2)

    def blocks(*lead):
        return [pltpu.VMEM((*lead, height, lanes), F32) for height in heights]

    def pieces(*lead):
        return [pltpu.VMEM((*lead, 2, height, lanes), F32) for height in heights[:2]] + [
            pltpu.VMEM((*lead, 2, height, lanes), F32) for height in heights[2:]
        ]

    scratch = [
        pltpu.VMEM((rows, rank), F32),
        pltpu.VMEM((rows, rank), F32),
        pltpu.VMEM((rows, 2 * rank), F32),
        pltpu.VMEM((rows, rank), F32),
        pltpu.VMEM((rows, rank), F32),
        pltpu.VMEM((rows, rank), F32),
        *blocks(2, NX, 4),
        *blocks(2, 2, 4),
        *blocks(2, 4),
        *pieces(4),
        *pieces(3),
        pltpu.VMEM((NX, NZ, 2 * rows_l, lanes), F32),
        pltpu.VMEM((NX, NZ, 2 * rows_l, lanes), F32),
        pltpu.VMEM((NZ, rows_q, lanes), F32),
        pltpu.VMEM((NZ, rows_q, lanes), F32),
        pltpu.VMEM((NX, 4, rows_q, lanes), F32),
        pltpu.VMEM((NX, 4, rows_q, lanes), F32),
        pltpu.VMEM((NX, 4, rows_q, lanes), F32),
        pltpu.SemaphoreType.DMA((6,)),
        pltpu.SemaphoreType.DMA((N_MESSAGES,)),
        pltpu.SemaphoreType.DMA((N_MESSAGES,)),
    ]
    out = jax.ShapeDtypeStruct((rows, rank), F32)
    return pl.pallas_call(
        kernel,
        out_shape=(out, out),
        in_specs=[pl.BlockSpec(memory_space=pl.ANY)] * 4,
        out_specs=[pl.BlockSpec(memory_space=pl.ANY)] * 2,
        scratch_shapes=scratch,
        compiler_params=pltpu.CompilerParams(collective_id=0, has_side_effects=True, vmem_limit_bytes=60 * 2**20),
        name="lowrank_level",
    )(low_solved, low_basis, upper_solved, upper_basis)


def solution(mesh):
    spec = P(("group", "leaf"), None)
    return jax.shard_map(
        body, mesh=mesh, in_specs=(spec,) * 4, out_specs=(spec,) * 2, check_vma=False
    )
```

time: 71.2 us -> 64.9 us (0.912)
  Pallas kernels: 67.6 us -> 61.4 us
    pallas_call x1, Pallas kernels: 67.6 us -> 61.4 us  [body(): pl.pallas_call(kernel, out_shape=(out, out), in_specs=[pl.BlockSpec(memor...]
where the time goes in v2:
time: 64.9 us; the launch traced here: 64.7 us
  Pallas kernels  61.4 us (95%)
  local copies, waits for them, and re-layouts  2.72 us (4%)
  between operations  0.65 us (1%)
    pallas_call x1, Pallas kernels, body(): pl.pallas_call(kernel, out_shape=(out, out), in_specs=[pl.BlockSpec(memor...  61.4 us
    unnamed x4, local copies, waits for them, and re-layouts  2.72 us

profile of v2, /device:TPU:1, one launch (start us, length us, event | category | flops | bytes accessed | tf_op | source)
XLA Modules:
  0.0 64.7 jit_solution(2190552334253581272)
XLA Ops:
  0.6 61.4 %lowrank_level.1 = (f32[512,256]{1,0:T(8,128)}, f32[512,256]{1,0:T(8,128)}) custom-call(f32[512,256]{1,0:T(8,128)} %y_hbm.1, f32[512,256]{1,0:T(8,128)} %v_hbm.1, f32[512,512]{1,0:T(8,128)} %z_hbm.1, f32[512,256]{1,0:T(8,128)} %w_hbm.1), custom_call_target="tpu_custom_call" | custom-call | tf_op jit(solution)/shard_map/lowrank_level/pallas_call | solution.py:402
  62.0 0.0 copy-start
  62.0 1.9 %copy.8 = f32[512,256]{1,0:T(8,128)} copy(f32[512,256]{1,0:T(8,128)} %get-tuple-element.4) | data formatting | bytes 1048576
  63.9 0.0 copy-done
  63.9 0.8 %copy.9 = f32[512,256]{1,0:T(8,128)} copy(f32[512,256]{1,0:T(8,128)S(1)} %copy-done) | data formatting | bytes 1048576
Async XLA Ops:
  62.0 1.9 %copy-start = (f32[512,256]{1,0:T(8,128)S(1)}, f32[512,256]{1,0:T(8,128)}, u32[]{:S(2)}) copy-start(f32[512,256]{1,0:T(8,128)} %get-tuple-element.5) | copy-start | bytes 1572868

commit v3 on v2

--- a/solution.py
+++ b/solution.py
@@ -17,8 +17,8 @@
 ORDER = (
     "CG", "xg", "CQ", "xq", "CP", "xg", "CS", "xp", "xq", "xs", "xg", "zg", "xp", "xq", "zq", "zg", "xs", "ag",
     "xp", "zp", "ag", "gn", "xs", "zs", "zp", "zq", "ap", "ag", "aq", "ap", "gn", "pn", "ap", "ag", "gr", "zs",
-    "as", "aq", "ap", "pr", "aq", "pn", "as", "as", "pr", "gr", "aq", "U", "as", "pr", "pn", "E", "fu", "ef",
-    "en", "fu", "M",
+    "as", "aq", "ap", "pr", "aq", "pn", "as", "as", "pr", "gr", "aq", "U", "as", "pr", "pn", "E", "fu", "en",
+    "ef", "W", "fu", "M",
 )
 
 
@@ -321,6 +321,17 @@
         held["e"][2].wait_recv()
         shared.append(send(full_e.at[far], sibling_e.at[far], across))
 
+    def solve_w():
+        for copy in shared:
+            copy.wait_recv()
+        b_own, r_own = split(joined(full_e, 0)), joined(full_e, 2)
+        b_sibling, r_sibling = split(joined(sibling_e, 0)), joined(sibling_e, 2)
+        update = r_own
+        update = r_sibling - dot3(b_sibling, split(update))
+        update = r_own - dot3(b_own, split(update))
+        update = r_sibling - dot3(b_sibling, split(update))
+        held["update"] = split(update)
+
     def middle():
         y_parts = split(y_ref[...])
         pair = z_ref[:, :rank] - dot3(y_parts, split(joined(full_u, 0)))
@@ -331,7 +342,7 @@
 
     actions = {
         "CG": compute_g, "CQ": compute_q, "CP": compute_p, "CS": compute_s,
-        "U": solve_u, "E": solve_e, "fu": lambda: run(flow_u), "en": near_e, "ef": far_e, "M": middle,
+        "U": solve_u, "E": solve_e, "fu": lambda: run(flow_u), "en": near_e, "ef": far_e, "M": middle, "W": solve_w,
     }
     flows = {
         "xg": xg, "xq": xq, "xp": xp, "xs": xs, "zg": [zg], "zq": [zq], "zp": [zp], "zs": [zs],
@@ -344,16 +355,8 @@
         else:
             run(*flows[token])
 
-    for copy in shared:
-        copy.wait_recv()
     pair, middle_next, pair_out = held["m"]
-    b_own, r_own = split(joined(full_e, 0)), joined(full_e, 2)
-    b_sibling, r_sibling = split(joined(sibling_e, 0)), joined(sibling_e, 2)
-    update = r_own
-    update = r_sibling - dot3(b_sibling, split(update))
-    update = r_own - dot3(b_own, split(update))
-    update = r_sibling - dot3(b_sibling, split(update))
-    next_ref[...] = middle_next - dot3(split(pair), split(update))
+    next_ref[...] = middle_next - dot3(split(pair), held["update"])
     next_out = pltpu.make_async_copy(next_ref, next_hbm, local_sem.at[5])
     next_out.start()
     for copy in sent:

time: 64.9 us -> 64.9 us (level)
  no operation moved by 1% of the time
where the time goes in v3:
time: 64.9 us; the launch traced here: 64.7 us
  Pallas kernels  61.4 us (95%)
  local copies, waits for them, and re-layouts  2.72 us (4%)
  between operations  0.65 us (1%)
    pallas_call x1, Pallas kernels, body(): pl.pallas_call(kernel, out_shape=(out, out), in_specs=[pl.BlockSpec(memor...  61.4 us
    unnamed x4, local copies, waits for them, and re-layouts  2.72 us

profile of v3, /device:TPU:1, one launch (start us, length us, event | category | flops | bytes accessed | tf_op | source)
XLA Modules:
  0.0 64.7 jit_solution(5242762952343843377)
XLA Ops:
  0.6 61.4 %lowrank_level.1 = (f32[512,256]{1,0:T(8,128)}, f32[512,256]{1,0:T(8,128)}) custom-call(f32[512,256]{1,0:T(8,128)} %y_hbm.1, f32[512,256]{1,0:T(8,128)} %v_hbm.1, f32[512,512]{1,0:T(8,128)} %z_hbm.1, f32[512,256]{1,0:T(8,128)} %w_hbm.1), custom_call_target="tpu_custom_call" | custom-call | tf_op jit(solution)/shard_map/lowrank_level/pallas_call | solution.py:405
  62.0 0.0 copy-start
  62.0 1.9 %copy.8 = f32[512,256]{1,0:T(8,128)} copy(f32[512,256]{1,0:T(8,128)} %get-tuple-element.4) | data formatting | bytes 1048576
  63.9 0.0 copy-done
  63.9 0.8 %copy.9 = f32[512,256]{1,0:T(8,128)} copy(f32[512,256]{1,0:T(8,128)S(1)} %copy-done) | data formatting | bytes 1048576
Async XLA Ops:
  62.0 1.9 %copy-start = (f32[512,256]{1,0:T(8,128)S(1)}, f32[512,256]{1,0:T(8,128)}, u32[]{:S(2)}) copy-start(f32[512,256]{1,0:T(8,128)} %get-tuple-element.5) | copy-start | bytes 1572868
